TPU v7x, 32 devices: a whole 2x2x4 slice. The times are simulated.
32 devices in a mesh: dp: 4 (over x, core), seq: 8 (over z, y).
Axes of the slice: x: 2, y: 2, z: 4, core: 2. Of those that a mesh axis runs over, the one named last changes fastest.
Arguments:
- tokens: bfloat16 [4, 4096, 1024], P('dp', 'seq'), may hold values from -6 to 6
- cotangent: bfloat16 [4, 4096, 1024], P('dp', 'seq'), may hold values from -6 to 6
- norm1_gain: float32 [1024], replicated, may hold values from 0.5 to 1.5
- norm1_bias: float32 [1024], replicated, may hold values from -1.25 to 1.25
- in_weight: bfloat16 [1024, 3072], replicated, may hold values from -0.1875 to 0.1875
- in_bias: float32 [3072], replicated, may hold values from -1.25 to 1.25
- short_weight: float32 [3, 3, 1024], P(None, None, 'seq'), may hold values from -3.5 to 3.5
- short_bias: float32 [3, 1024], P(None, 'seq'), may hold values from -1.25 to 1.25
- filter_in: float32 [33, 64], replicated, may hold values from -2 to 2
- filter_in_bias: float32 [64], replicated, may hold values from -3 to 3
- sine_freq: float32 [64], replicated, may hold values from 0.5 to 2
- filter_out: float32 [64, 1024], P(None, 'seq'), may hold values from -0.03125 to 0.03125
- decay_rates: float32 [1024], P('seq'), may hold values from 2 to 64
- filter_bias: float32 [1024], P('seq'), may hold values from -6 to 6
- out_weight: bfloat16 [1024, 1024], replicated, may hold values from -0.1875 to 0.1875
- out_bias: float32 [1024], replicated, may hold values from -1.25 to 1.25
- norm2_gain: float32 [1024], replicated, may hold values from 0.5 to 1.5
- norm2_bias: float32 [1024], replicated, may hold values from -1.25 to 1.25
- up_weight: bfloat16 [1024, 4096], replicated, may hold values from -0.1875 to 0.1875
- up_bias: float32 [4096], replicated, may hold values from -1.25 to 1.25
- down_weight: bfloat16 [4096, 1024], replicated, may hold values from -0.125 to 0.125
- down_bias: float32 [1024], replicated, may hold values from -1.25 to 1.25
Outputs:
- block_output: bfloat16 [4, 4096, 1024], P('dp', 'seq')
- grad_tokens: float32 [4, 4096, 1024], P('dp', 'seq')
- grad_norm1_gain: float32 [1024], replicated
- grad_norm1_bias: float32 [1024], replicated
- grad_in_weight: float32 [1024, 3072], P('seq', 'dp')
- grad_in_bias: float32 [3072], replicated
- grad_short_weight: float32 [3, 3, 1024], P(None, None, 'seq')
- grad_short_bias: float32 [3, 1024], P(None, 'seq')
- grad_filter_in: float32 [33, 64], replicated
- grad_filter_in_bias: float32 [64], replicated
- grad_sine_freq: float32 [64], replicated
- grad_filter_out: float32 [64, 1024], P(None, 'seq')
- grad_filter_bias: float32 [1024], P('seq')
- grad_out_weight: float32 [1024, 1024], P('seq', 'dp')
- grad_out_bias: float32 [1024], replicated
- grad_norm2_gain: float32 [1024], replicated
- grad_norm2_bias: float32 [1024], replicated
- grad_up_weight: float32 [1024, 4096], P('seq', 'dp')
- grad_up_bias: float32 [4096], replicated
- grad_down_weight: float32 [4096, 1024], P('seq', 'dp')
- grad_down_bias: float32 [1024], replicated
All inputs are finite; a program needn't handle non-finite values.
Results may differ from a plain program's by a relative error of at most 0.014.
Values may be sent and summed in bfloat16 or wider, within the bound.
No kernel may reach another device: no remote copies, remote signals or barrier semaphores. Data moves between devices by JAX's collectives and lax.ppermute only.
A program may use at most 320 MiB of HBM per device.

v0:
```python
import math
import jax
import jax.numpy as jnp
from jax import lax
from jax.sharding import PartitionSpec as P

EMB = 33
HIGH = lax.Precision.HIGHEST
EPSILON = 1e-05


def layer_norm(values, scale_vec, shift_vec):
    average = jnp.mean(values, axis=-1, keepdims=True)
    centred = values - average
    variance = jnp.mean(centred * centred, axis=-1, keepdims=True)
    return centred * lax.rsqrt(variance + EPSILON) * scale_vec + shift_vec


def position_features(length):
    steps = jnp.arange(length, dtype=jnp.float32)
    scaled = steps / (length - 1)
    angles = 2.0 * math.pi * steps / length
    bands = (EMB - 1) // 2
    freqs = 0.0001 + jnp.arange(bands, dtype=jnp.float32) * (bands - 1 - 0.0001) / (bands - 1)
    phase = freqs[:, None] * angles[None, :]
    return jnp.concatenate([scaled[None, :], jnp.cos(phase), -jnp.sin(phase)], axis=0)


def make_filter(filter_in, in_shift, sine_freq, filter_out, decay_rates, features):
    hidden_pre = jnp.dot(filter_in.T, features, precision=HIGH) + in_shift[:, None]
    hidden = jnp.sin(sine_freq[:, None] * hidden_pre)
    raw_kernel = jnp.dot(filter_out.T, hidden, precision=HIGH)
    return raw_kernel * jnp.exp(-decay_rates[:, None] * features[0][None, :])


def split_length(full_length):
    leading = 2
    while leading * leading * 2 <= full_length and full_length % (leading * 2) == 0:
        leading = leading * 2
    return (leading, full_length // leading)


def dft_tables(count_p, count_q):
    full_length = count_p * count_q
    index_p = jnp.arange(count_p, dtype=jnp.int32)
    index_q = jnp.arange(count_q, dtype=jnp.int32)
    prod_p = index_p[:, None] * index_p[None, :] % count_p
    prod_q = index_q[:, None] * index_q[None, :] % count_q
    prod_t = index_p[:, None] * index_q[None, :] % full_length
    angle_p = 2.0 * math.pi * prod_p.astype(jnp.float32) / count_p
    angle_q = 2.0 * math.pi * prod_q.astype(jnp.float32) / count_q
    angle_t = 2.0 * math.pi * prod_t.astype(jnp.float32) / full_length
    return (
        jnp.cos(angle_p),
        jnp.sin(angle_p),
        jnp.cos(angle_q),
        jnp.sin(angle_q),
        jnp.cos(angle_t),
        jnp.sin(angle_t),
    )


def forward_real(signal, tables):
    cos_p, sin_p, cos_q, sin_q, cos_t, sin_t = tables
    half_rows = cos_p.shape[0] // 2
    count_q = cos_q.shape[0]
    blocked = signal.reshape(signal.shape[0], half_rows, count_q)
    part_re = jnp.einsum("kn,cnq->ckq", cos_p[:, :half_rows], blocked, precision=HIGH)
    part_im = -jnp.einsum("kn,cnq->ckq", sin_p[:, :half_rows], blocked, precision=HIGH)
    turned_re = part_re * cos_t + part_im * sin_t
    turned_im = part_im * cos_t - part_re * sin_t
    spec_re = jnp.einsum("ckn,nm->ckm", turned_re, cos_q, precision=HIGH) + jnp.einsum(
        "ckn,nm->ckm", turned_im, sin_q, precision=HIGH
    )
    spec_im = jnp.einsum("ckn,nm->ckm", turned_im, cos_q, precision=HIGH) - jnp.einsum(
        "ckn,nm->ckm", turned_re, sin_q, precision=HIGH
    )
    return (spec_re, spec_im)


def inverse_real(spec_re, spec_im, tables):
    cos_p, sin_p, cos_q, sin_q, cos_t, sin_t = tables
    half_rows = cos_p.shape[0] // 2
    full_length = cos_p.shape[0] * cos_q.shape[0]
    back_re = jnp.einsum("ckm,nm->ckn", spec_re, cos_q, precision=HIGH) - jnp.einsum(
        "ckm,nm->ckn", spec_im, sin_q, precision=HIGH
    )
    back_im = jnp.einsum("ckm,nm->ckn", spec_im, cos_q, precision=HIGH) + jnp.einsum(
        "ckm,nm->ckn", spec_re, sin_q, precision=HIGH
    )
    twist_re = back_re * cos_t - back_im * sin_t
    twist_im = back_im * cos_t + back_re * sin_t
    result = jnp.einsum("nk,ckq->cnq", cos_p[:half_rows], twist_re, precision=HIGH) - jnp.einsum(
        "nk,ckq->cnq", sin_p[:half_rows], twist_im, precision=HIGH
    )
    return result.reshape(spec_re.shape[0], full_length // 2) / full_length


def mixer(
    received,
    short_taps,
    tap_shift,
    filter_in,
    in_shift,
    sine_freq,
    filter_out,
    filter_shift,
    decay_rates,
    features,
    tables,
):
    length = received.shape[2]
    shifted_one = jnp.pad(received, ((0, 0), (0, 0), (1, 0)))[:, :, :length]
    shifted_two = jnp.pad(received, ((0, 0), (0, 0), (2, 0)))[:, :, :length]
    short = (
        tap_shift[:, :, None]
        + short_taps[0][:, :, None] * shifted_two
        + short_taps[1][:, :, None] * shifted_one
        + short_taps[2][:, :, None] * received
    )
    gate_out, gate_in, values = (short[0], short[1], short[2])
    kernel = make_filter(filter_in, in_shift, sine_freq, filter_out, decay_rates, features)
    inner = values * gate_in
    inner_re, inner_im = forward_real(inner, tables)
    kernel_re, kernel_im = forward_real(kernel, tables)
    conv = inverse_real(
        inner_re * kernel_re - inner_im * kernel_im,
        inner_re * kernel_im + inner_im * kernel_re,
        tables,
    )
    conv = conv + inner * filter_shift[:, None]
    return conv * gate_out


def reduce_matrices(matrix_grads):
    partial_sums = (
        lax.psum_scatter(matrix_grads[0], "seq", scatter_dimension=0, tiled=True),
        lax.psum_scatter(matrix_grads[1], "seq", scatter_dimension=0, tiled=True),
        lax.psum_scatter(matrix_grads[2], "seq", scatter_dimension=0, tiled=True),
        lax.psum_scatter(matrix_grads[3], "seq", scatter_dimension=0, tiled=True),
    )
    reduced = (
        lax.psum_scatter(partial_sums[0], "dp", scatter_dimension=1, tiled=True),
        lax.psum_scatter(partial_sums[1], "dp", scatter_dimension=1, tiled=True),
        lax.psum_scatter(partial_sums[2], "dp", scatter_dimension=1, tiled=True),
        lax.psum_scatter(partial_sums[3], "dp", scatter_dimension=1, tiled=True),
    )
    return reduced


def on_device(
    tokens,
    cotangent,
    norm1_gain,
    norm1_bias,
    in_weight,
    in_bias,
    short_weight,
    short_bias,
    filter_in,
    filter_in_bias,
    sine_freq,
    filter_out,
    decay_rates,
    filter_bias,
    out_weight,
    out_bias,
    norm2_gain,
    norm2_bias,
    up_weight,
    up_bias,
    down_weight,
    down_bias,
):
    model_width = in_weight.shape[0]
    tok_rows = tokens.shape[1]
    group_size = lax.axis_size("seq")
    length = tok_rows * group_size
    local_tokens = tokens[0].astype(jnp.float32)
    normed, norm1_pull = jax.vjp(layer_norm, local_tokens, norm1_gain, norm1_bias)
    normed_low = normed.astype(jnp.bfloat16)
    in_three = in_weight.reshape(model_width, 3, model_width)
    projected = jnp.einsum("td,dkc->kct", normed_low, in_three, preferred_element_type=jnp.float32)
    projected = projected + in_bias.reshape(3, model_width)[:, :, None]
    received = lax.all_to_all(
        projected.astype(jnp.bfloat16), "seq", split_axis=1, concat_axis=2, tiled=True
    )
    features = position_features(length)
    count_p, count_q = split_length(2 * length)
    tables = dft_tables(count_p, count_q)

    def local_mixer(
        recv_values, taps, tap_shift, first_layer, first_shift, freqs, last_layer, direct_shift
    ):
        return mixer(
            recv_values,
            taps,
            tap_shift,
            first_layer,
            first_shift,
            freqs,
            last_layer,
            direct_shift,
            decay_rates,
            features,
            tables,
        )

    mixed, mixer_pull = jax.vjp(
        local_mixer,
        received.astype(jnp.float32),
        short_weight,
        short_bias,
        filter_in,
        filter_in_bias,
        sine_freq,
        filter_out,
        filter_bias,
    )
    returned = lax.all_to_all(
        mixed.astype(jnp.bfloat16), "seq", split_axis=1, concat_axis=0, tiled=True
    )
    attended = (
        jnp.einsum("ct,ce->te", returned, out_weight, preferred_element_type=jnp.float32) + out_bias
    )
    resid = local_tokens + attended
    normed2, norm2_pull = jax.vjp(layer_norm, resid, norm2_gain, norm2_bias)
    normed2_low = normed2.astype(jnp.bfloat16)
    up_pre = jnp.dot(normed2_low, up_weight, preferred_element_type=jnp.float32) + up_bias
    activated, gelu_pull = jax.vjp(jax.nn.gelu, up_pre)
    activated_low = activated.astype(jnp.bfloat16)
    block_out = (
        resid + jnp.dot(activated_low, down_weight, preferred_element_type=jnp.float32) + down_bias
    )
    grad_out = cotangent[0]
    grad_down = jnp.einsum("tf,td->fd", activated_low, grad_out, preferred_element_type=jnp.float32)
    grad_down_bias = jnp.sum(grad_out.astype(jnp.float32), axis=0)
    grad_activated = jnp.einsum(
        "td,fd->tf", grad_out, down_weight, preferred_element_type=jnp.float32
    )
    grad_up_pre = gelu_pull(grad_activated)[0].astype(jnp.bfloat16)
    grad_up = jnp.einsum("td,tf->df", normed2_low, grad_up_pre, preferred_element_type=jnp.float32)
    grad_up_bias = jnp.sum(grad_up_pre.astype(jnp.float32), axis=0)
    grad_normed2 = jnp.einsum(
        "tf,df->td", grad_up_pre, up_weight, preferred_element_type=jnp.float32
    )
    grad_resid_norm, grad_gain2, grad_shift2 = norm2_pull(grad_normed2)
    grad_resid = grad_out.astype(jnp.float32) + grad_resid_norm
    grad_attn = grad_resid.astype(jnp.bfloat16)
    grad_out_weight = jnp.einsum(
        "ct,te->ce", returned, grad_attn, preferred_element_type=jnp.float32
    )
    grad_out_bias = jnp.sum(grad_attn.astype(jnp.float32), axis=0)
    grad_mixed_rows = jnp.einsum(
        "te,ce->ct", grad_attn, out_weight, preferred_element_type=jnp.float32
    )
    grad_mixed = lax.all_to_all(
        grad_mixed_rows.astype(jnp.bfloat16), "seq", split_axis=0, concat_axis=1, tiled=True
    )
    (
        grad_received,
        grad_taps,
        grad_tap_shift,
        grad_first,
        grad_first_shift,
        grad_freqs,
        grad_last,
        grad_direct,
    ) = mixer_pull(grad_mixed.astype(jnp.float32))
    grad_proj = lax.all_to_all(
        grad_received.astype(jnp.bfloat16), "seq", split_axis=2, concat_axis=1, tiled=True
    )
    grad_in = jnp.einsum("td,kct->dkc", normed_low, grad_proj, preferred_element_type=jnp.float32)
    grad_in = grad_in.reshape(model_width, 3 * model_width)
    grad_in_bias = jnp.sum(grad_proj.astype(jnp.float32), axis=2).reshape(3 * model_width)
    grad_normed = jnp.einsum("kct,dkc->td", grad_proj, in_three, preferred_element_type=jnp.float32)
    grad_tokens_norm, grad_gain1, grad_shift1 = norm1_pull(grad_normed)
    grad_tokens = grad_resid + grad_tokens_norm
    matrix_sums = reduce_matrices((grad_in, grad_out_weight, grad_up, grad_down))
    shared = lax.psum(
        (
            grad_gain1,
            grad_shift1,
            grad_in_bias,
            grad_out_bias,
            grad_gain2,
            grad_shift2,
            grad_up_bias,
            grad_down_bias,
            grad_first,
            grad_first_shift,
            grad_freqs,
        ),
        ("dp", "seq"),
    )
    channel = lax.psum((grad_taps, grad_tap_shift, grad_last, grad_direct), "dp")
    return (
        block_out.astype(jnp.bfloat16)[None],
        grad_tokens[None],
        shared[0],
        shared[1],
        matrix_sums[0],
        shared[2],
        channel[0],
        channel[1],
        shared[8],
        shared[9],
        shared[10],
        channel[2],
        channel[3],
        matrix_sums[1],
        shared[3],
        shared[4],
        shared[5],
        matrix_sums[2],
        shared[6],
        matrix_sums[3],
        shared[7],
    )


def solution(mesh):
    in_specs = (
        P("dp", "seq", None),
        P("dp", "seq", None),
        P(),
        P(),
        P(),
        P(),
        P(None, None, "seq"),
        P(None, "seq"),
        P(),
        P(),
        P(),
        P(None, "seq"),
        P("seq"),
        P("seq"),
        P(),
        P(),
        P(),
        P(),
        P(),
        P(),
        P(),
        P(),
    )
    out_specs = (
        P("dp", "seq", None),
        P("dp", "seq", None),
        P(),
        P(),
        P("seq", "dp"),
        P(),
        P(None, None, "seq"),
        P(None, "seq"),
        P(),
        P(),
        P(),
        P(None, "seq"),
        P("seq"),
        P("seq", "dp"),
        P(),
        P(),
        P(),
        P("seq", "dp"),
        P(),
        P("seq", "dp"),
        P(),
    )
    return jax.shard_map(
        on_device, mesh=mesh, in_specs=in_specs, out_specs=out_specs, check_vma=False
    )
```

profile of v0, /device:TPU:0, one launch (start us, length us, event | category | flops | bytes accessed | tf_op | source)
XLA Modules:
  0.0 1629.9 jit_solution(7584546690204504811)
XLA Ops:
  56.7 9.5 fusion.128
  66.2 70.4 %all-to-all-done = bf16[3,1024,512]{2,0,1:T(4,128)(2,1)} async-done(((bf16[3,1024,512]{2,0,1:T(4,128)(2,1)}), bf16[3,1024,512]{2,0,1:T(4,128)(2,1)}, u32[]{:S(2)}, u32[]{:S(2)}) %all-to-all-start) | async-done | bytes 3145760 | tf_op jit(solution)/shard_map/all_to_all | solution.py:185
  160.5 9.3 fusion.132
  169.9 9.6 fusion.134
  179.4 12.3 fusion.24
  211.7 9.2 fusion.64
  220.9 9.6 fusion.88
  230.5 9.1 fusion.91
  239.6 9.4 fusion.82
  249.0 14.2 multiply_subtract_fusion
  280.8 18.1 %fusion.44 = f32[128,64,64]{0,2,1:T(8,128)S(1)} fusion(f32[128,64]{0,1:T(8,128)S(1)} %get-tuple-element.104, f32[128,64]{0,1:T(8,128)S(1)} %get-tuple-element.105, f32[128,128,64]{1,2,0:T(8,128)S(1)} %fusion.185, f32[128,128,64]{1,2,0:T(8,128)S(1)} %fusion.203, f32[128,128,64]{1,2,0:T(8,128)S(1)} %fusion.183, f32[128,128,64]{1,2,0:T(8,128)S(1)} %fusion.201, ...), kind=kOutput, calls=%fused_computation.89 | convolution fusion | flops 810549248 | bytes 19005440 | tf_op jit(solution)/shard_map/jvp(nk,ckq->cnq)/dot_general | solution.py:93
  298.9 21.2 %multiply_bitcast_fusion = f32[128,64,64]{0,1,2:T(8,128)S(1)} fusion(f32[128,64,64]{0,2,1:T(8,128)S(1)} %fusion.44, f32[128,64]{0,1:T(8,128)S(1)} %get-tuple-element.104, f32[128,64]{0,1:T(8,128)S(1)} %get-tuple-element.105, f32[128,128,64]{1,2,0:T(8,128)S(1)} %fusion.185, f32[128,128,64]{1,2,0:T(8,128)S(1)} %fusion.203, f32[128,128,64]{1,2,0:T(8,128)S(1)} %fusion.183, ...), kind=kOutput, calls=%fused_computation.185 | convolution fusion | flops 811597824 | bytes 21102592 | tf_op jit(solution)/shard_map/jvp(nk,ckq->cnq)/dot_general | solution.py:93
  322.0 29.5 %all_to_all.56 = bf16[128,8,512]{0,2,1:T(8,128)(2,1)} all-to-all(bf16[128,8,512]{0,2,1:T(8,128)(2,1)S(1)} %fusion.119), channel_id=1, replica_groups=mesh['dp'=4,'seq'=8] {'seq'}, dimensions={1} | all-to-all | bytes 2097152 | tf_op jit(solution)/shard_map/all_to_all | solution.py:220
  356.8 10.8 fusion.354
  367.6 16.2 convert_reduce_fusion
  405.5 36.1 %all-to-all-done.2 = bf16[8,128,512]{1,2,0:T(8,128)(2,1)} async-done(((bf16[8,128,512]{1,2,0:T(8,128)(2,1)}), bf16[8,128,512]{1,2,0:T(8,128)(2,1)}, u32[]{:S(2)}, u32[]{:S(2)}) %all-to-all-start.2) | async-done | bytes 1048608 | tf_op jit(solution)/shard_map/all_to_all | solution.py:257
  466.6 9.6 fusion.38
  476.2 9.3 fusion.97
  485.5 17.6 %multiply_add_fusion.2 = (f32[128,128,64]{1,2,0:T(8,128)S(1)}, f32[128,128,64]{1,2,0:T(8,128)}, f32[128,128,64]{1,2,0:T(8,128)}, f32[128,128,64]{1,2,0:T(8,128)}) fusion(f32[128,128,64]{1,2,0:T(8,128)} %get-tuple-element.96, f32[128,128,64]{1,2,0:T(8,128)} %fusion.82, f32[128,128,64]{1,2,0:T(8,128)} %fusion.97, f32[128,128,64]{1,2,0:T(8,128)} %fusion.88, ...), kind=kOutput, calls=%fused_computation.84 | convolution fusion | flops 820043776 | bytes 46137344 | tf_op jit(solution)/shard_map/transpose(jvp(ckm,nm->ckn))/dot_general | solution.py:88
  538.8 12.2 fusion.14
  551.0 9.3 fusion.32
  589.9 20.0 %copy.246 = bf16[3,128,4096]{1,0,2:T(4,128)(2,1)S(1)} copy(bf16[3,128,4096]{1,2,0:T(8,128)(2,1)S(1)} %fusion.9) | data formatting | bytes 6291456 | tf_op jit(solution)/shard_map/convert_element_type | solution.py:271
  609.9 93.2 %all_to_all.57 = bf16[3,128,4096]{1,0,2:T(4,128)(2,1)S(1)} all-to-all(bf16[3,128,4096]{1,0,2:T(4,128)(2,1)S(1)} %copy.246), channel_id=1, replica_groups=mesh['dp'=4,'seq'=8] {'seq'}, dimensions={2} | all-to-all | bytes 6291456 | tf_op jit(solution)/shard_map/all_to_all | solution.py:270
  719.1 13.3 fusion.353
  732.5 15.8 fusion.145
  748.9 176.9 %reduce-scatter.9.cloned.1.call-done = f32[128,3072]{1,0:T(8,128)} async-done(((f32[1024,3072]{1,0:T(8,128)}), f32[128,3072]{1,0:T(8,128)}) %reduce-scatter.9.cloned.1.call-update) | async-done | bytes 1572880 | tf_op jit(solution)/shard_map/reduce_scatter | solution.py:137
  925.9 286.0 %reduce-scatter.17.cloned.1.call-done = f32[128,4096]{1,0:T(8,128)} async-done(((f32[1024,4096]{1,0:T(8,128)}), f32[128,4096]{1,0:T(8,128)}) %reduce-scatter.17.cloned.1.call-update) | async-done | bytes 2097168 | tf_op jit(solution)/shard_map/reduce_scatter | solution.py:139
  1212.2 13.0 fusion.143
  1242.0 255.4 %reduce-scatter.21.cloned.1.call-done = f32[512,1024]{1,0:T(8,128)} async-done(((f32[4096,1024]{1,0:T(8,128)}), f32[512,1024]{1,0:T(8,128)}) %reduce-scatter.21.cloned.1.call-update) | async-done | bytes 2097168 | tf_op jit(solution)/shard_map/reduce_scatter | solution.py:140
  1510.1 12.6 all-reduce.11
  1541.1 41.1 %all-reduce.10 = (f32[1024]{0:T(1024)}, f32[1024]{0:T(1024)}, f32[3072]{0:T(1024)}, f32[33,64]{1,0:T(8,128)}, f32[64]{0:T(128)}, /*index=5*/f32[64]{0:T(128)}, f...) all-reduce(f32[1024]{0:T(1024)S(1)} %get-tuple-element.29, ...), channel_id=1, replica_groups=mesh['dp'=4,'seq'=8] {'dp','seq'}, use_global_device_ids=true, to_apply=%region_9.10 | all-reduce | flops 15552 | bytes 124416 | tf_op jit(solution)/shard_map/psum | solution.py:280
  1588.3 34.5 %reduce-scatter.23.cloned.1.call-done = f32[512,256]{1,0:T(8,128)} async-done(((f32[512,1024]{1,0:T(8,128)}), f32[512,256]{1,0:T(8,128)}) %reduce-scatter.23.cloned.1.call-update) | async-done | bytes 524304 | tf_op jit(solution)/shard_map/reduce_scatter | solution.py:146
  (276 shorter events, 300.0 us)
Async XLA Ops:
  7.2 346.6 %copy-start = (bf16[1024,1024]{1,0:T(8,128)(2,1)S(1)}, bf16[1024,1024]{1,0:T(8,128)(2,1)}, u32[]{:S(2)}) copy-start(bf16[1024,1024]{1,0:T(8,128)(2,1)} %param.36) | copy-start | bytes 6291460
  35.4 101.2 %all-to-all-start = ((bf16[3,1024,512]{2,0,1:T(4,128)(2,1)}), bf16[3,1024,512]{2,0,1:T(4,128)(2,1)}, u32[]{:S(2)}, u32[]{:S(2)}) async-start(bf16[3,1024,512]{2,0,1:T(4,128)(2,1)} %copy.198), calls=%async_computation | async-start | bytes 8388608 | tf_op jit(solution)/shard_map/all_to_all | solution.py:185
  44.2 105.5 %copy-start.50 = (f32[3,128]{1,0:T(4,128)}, f32[3,128]{1,0:T(4,128)S(1)}, u32[]{:S(2)}) copy-start(f32[3,128]{1,0:T(4,128)S(1)} %get-tuple-element.94) | copy-start | bytes 4612
  44.3 105.5 %copy-start.52 = (f32[3,128]{1,0:T(4,128)}, f32[3,128]{1,0:T(4,128)S(1)}, u32[]{:S(2)}) copy-start(f32[3,128]{1,0:T(4,128)S(1)} %get-tuple-element.93) | copy-start | bytes 4612
  44.3 105.5 %copy-start.54 = (f32[3,128]{1,0:T(4,128)}, f32[3,128]{1,0:T(4,128)S(1)}, u32[]{:S(2)}) copy-start(f32[3,128]{1,0:T(4,128)S(1)} %get-tuple-element.95) | copy-start | bytes 4612
  160.5 160.8 %copy-start.2 = (f32[1,128,4096]{1,2,0:T(8,128)}, f32[1,128,4096]{1,2,0:T(8,128)S(1)}, u32[]{:S(2)}) copy-start(f32[1,128,4096]{1,2,0:T(8,128)S(1)} %get-tuple-element.80) | copy-start | bytes 6291460
  321.3 30.1 %copy-start.17 = (f32[128,64,64]{0,2,1:T(8,128)}, f32[128,64,64]{0,2,1:T(8,128)S(1)}, u32[]{:S(2)}) copy-start(f32[128,64,64]{0,2,1:T(8,128)S(1)} %copy.227) | copy-start | bytes 6291460
  321.7 32.1 %copy-start.40 = (f32[1024]{0:T(1024)S(1)}, f32[1024]{0:T(1024)}, u32[]{:S(2)}) copy-start(f32[1024]{0:T(1024)} %param.37) | copy-start | bytes 12292
  356.4 35.5 %copy-start.14 = (f32[512,1024]{1,0:T(8,128)}, f32[512,1024]{1,0:T(8,128)S(1)}, u32[]{:S(2)}) copy-start(f32[512,1024]{1,0:T(8,128)S(1)} %get-tuple-element.98) | copy-start | bytes 6291460
  356.8 27.0 %slice-start.4 = ((s8[8388608]{0:T(1024)(128)(4,1)}), s8[4194304]{0:T(1024)(128)(4,1)S(1)}, s32[]{:S(2)}) async-start(s8[8388608]{0:T(1024)(128)(4,1)} %bitcast.400), calls=%async_computation.24 | async-start | bytes 8388608
  367.6 16.2 slice-start.5
  396.4 45.3 %all-to-all-start.2 = ((bf16[8,128,512]{1,2,0:T(8,128)(2,1)}), bf16[8,128,512]{1,2,0:T(8,128)(2,1)}, u32[]{:S(2)}, u32[]{:S(2)}) async-start(bf16[8,128,512]{1,2,0:T(8,128)(2,1)} %bitcast.369), calls=%async_computation.2 | async-start | bytes 2097152 | tf_op jit(solution)/shard_map/all_to_all | solution.py:257
  400.6 347.7 %reduce-scatter.13.cloned.1.call-start = ((), (), s32[]{:S(2)}) async-start(), calls=%async_computation.14 | async-start | bytes 4718592 | tf_op jit(solution)/shard_map/reduce_scatter | solution.py:138
  405.3 37.7 %copy-start.16 = (f32[1,128,4096]{1,2,0:T(8,128)S(1)}, f32[1,128,4096]{1,2,0:T(8,128)}, u32[]{:S(2)}) copy-start(f32[1,128,4096]{1,2,0:T(8,128)} %get-tuple-element.81) | copy-start | bytes 6291460
  405.3 520.5 %reduce-scatter.9.cloned.1.call-start = ((), (), s32[]{:S(2)}) async-start(), calls=%async_computation.12 | async-start | bytes 14155776 | tf_op jit(solution)/shard_map/reduce_scatter | solution.py:137
  459.9 16.3 %copy-start.8 = (f32[128,128,64]{1,0,2:T(8,128)}, f32[128,128,64]{1,0,2:T(8,128)S(1)}, u32[]{:S(2)}) copy-start(f32[128,128,64]{1,0,2:T(8,128)S(1)} %get-tuple-element.71) | copy-start | bytes 12582916
  551.0 18.9 %slice-start.2 = ((s8[6291456]{0:T(1024)(128)(4,1)}), s8[4194304]{0:T(1024)(128)(4,1)S(1)}, s32[]{:S(2)}) async-start(s8[6291456]{0:T(1024)(128)(4,1)} %bitcast.378), calls=%async_computation.22 | async-start | bytes 8388608
  719.1 492.8 %reduce-scatter.17.cloned.1.call-start = ((), (), s32[]{:S(2)}) async-start(), calls=%async_computation.16 | async-start | bytes 18874368 | tf_op jit(solution)/shard_map/reduce_scatter | solution.py:139
  732.5 764.9 %reduce-scatter.21.cloned.1.call-start = ((), (), s32[]{:S(2)}) async-start(), calls=%async_computation.18 | async-start | bytes 18874368 | tf_op jit(solution)/shard_map/reduce_scatter | solution.py:140
  748.3 463.8 %copy-start.76 = (f32[1024]{0:T(1024)S(1)}, f32[1024]{0:T(1024)}, u32[]{:S(2)}) copy-start(f32[1024]{0:T(1024)} %param.43) | copy-start | bytes 12292
  748.3 833.9 %reduce-scatter.15.cloned.1.call-start = ((), (), s32[]{:S(2)}) async-start(), calls=%async_computation.15 | async-start | bytes 655360 | tf_op jit(solution)/shard_map/reduce_scatter | solution.py:144
  748.9 833.3 %reduce-scatter.11.cloned.1.call-start = ((), (), s32[]{:S(2)}) async-start(), calls=%async_computation.13 | async-start | bytes 1966080 | tf_op jit(solution)/shard_map/reduce_scatter | solution.py:143
  925.9 662.5 %reduce-scatter.19.cloned.1.call-start = ((), (), s32[]{:S(2)}) async-start(), calls=%async_computation.17 | async-start | bytes 2621440 | tf_op jit(solution)/shard_map/reduce_scatter | solution.py:145
  1211.9 410.9 %reduce-scatter.23.cloned.1.call-start = ((), (), s32[]{:S(2)}) async-start(), calls=%async_computation.19 | async-start | bytes 2621440 | tf_op jit(solution)/shard_map/reduce_scatter | solution.py:146
  1239.4 258.0 %copy-start.37 = (f32[4096]{0:T(1024)S(1)}, f32[4096]{0:T(1024)}, u32[]{:S(2)}) copy-start(f32[4096]{0:T(1024)} %copy-done.36) | copy-start | bytes 49156
  1239.4 258.0 %copy-start.68 = (f32[128]{0:T(128)S(1)}, f32[128]{0:T(128)}, u32[]{:S(2)}) copy-start(f32[128]{0:T(128)} %copy-done.67) | copy-start | bytes 1540
  1241.9 258.8 %copy-start.62 = (f32[64]{0:T(128)S(1)}, f32[64]{0:T(128)}, u32[]{:S(2)}) copy-start(f32[64]{0:T(128)} %param.32) | copy-start | bytes 772
  1500.8 21.9 %copy-start.39 = (f32[64,128]{1,0:T(8,128)S(1)}, f32[64,128]{1,0:T(8,128)}, u32[]{:S(2)}) copy-start(f32[64,128]{1,0:T(8,128)} %param.33) | copy-start | bytes 98308
  1507.5 22.6 %copy-start.30 = (f32[16,4096]{1,0:T(8,128)S(1)}, f32[16,4096]{1,0:T(8,128)}, u32[]{:S(2)}) copy-start(f32[16,4096]{1,0:T(8,128)} %copy-done.29) | copy-start | bytes 786436
  1507.5 22.6 %copy-start.35 = (f32[1,4096]{1,0:T(1,128)S(1)}, f32[1,4096]{1,0:T(1,128)}, u32[]{:S(2)}) copy-start(f32[1,4096]{1,0:T(1,128)} %copy-done.34) | copy-start | bytes 49156
  1510.1 20.0 %copy-start.32 = (f32[16,4096]{1,0:T(8,128)S(1)}, f32[16,4096]{1,0:T(8,128)}, u32[]{:S(2)}) copy-start(f32[16,4096]{1,0:T(8,128)} %copy-done.31) | copy-start | bytes 786436
  1538.3 84.5 %copy-start.1 = (bf16[1024,1024]{1,0:T(8,128)(2,1)S(1)}, bf16[1024,1024]{1,0:T(8,128)(2,1)}, u32[]{:S(2)}) copy-start(bf16[1024,1024]{1,0:T(8,128)(2,1)} %param.36) | copy-start | bytes 6291460
  (62 other events, 348.5 us)
Sparse Core Ops, SparseCore 0:
  405.4 97.9 reduce-scatter.12
  719.2 206.5 reduce-scatter.8
  930.1 281.7 reduce-scatter.16
  1215.5 281.7 reduce-scatter.20
  1500.4 21.0 reduce-scatter.14
  1524.4 28.4 reduce-scatter.10
  1556.2 32.0 reduce-scatter.18
  1591.4 31.3 reduce-scatter.22
where the time goes:
time: 1630 us
  waiting for transfers between devices  866 us (53%)
  matrix products  437 us (27%)
  blocking collectives  176 us (11%)
  local copies, waits for them, and re-layouts  68.8 us (4%)
  other arithmetic  52.5 us (3%)
    reduce_scatter x1, waiting for transfers between devices, reduce_matrices(): lax.psum_scatter(matrix_grads[2], 'seq', scatter_dimension=0, tiled=True)  286 us
    reduce_scatter x1, waiting for transfers between devices, reduce_matrices(): lax.psum_scatter(matrix_grads[3], 'seq', scatter_dimension=0, tiled=True)  255 us
    reduce_scatter x1, waiting for transfers between devices, reduce_matrices(): lax.psum_scatter(matrix_grads[0], 'seq', scatter_dimension=0, tiled=True)  177 us
    all_to_all x1, blocking collectives, on_device(): lax.all_to_all(grad_received.astype(jnp.bfloat16), 'seq', split_axis=2, c...  93.2 us
    all_to_all x1, waiting for transfers between devices, on_device(): lax.all_to_all(projected.astype(jnp.bfloat16), 'seq', split_axis=1, conca...  70.4 us
    dot_general x4, matrix products, forward_real(): jnp.einsum('ckn,nm->ckm', turned_re, sin_q, precision=HIGH)  41.6 us
    psum x1, blocking collectives, on_device(): lax.psum((grad_gain1, grad_shift1, grad_in_bias, grad_out_bias, grad_gain...  41.1 us
    dot_general x4, matrix products, forward_real(): jnp.einsum('kn,cnq->ckq', cos_p[:, :half_rows], blocked, precision=HIGH)  38.2 us
  transfers between devices with their start and end apart: 10, of which 7 were waited for; matrix products, arithmetic and copies ran while one was open for 18% of the time, Pallas kernels for 0%

commit v1 on v0

--- a/solution.py
+++ b/solution.py
@@ -182,9 +182,20 @@
     in_three = in_weight.reshape(model_width, 3, model_width)
     projected = jnp.einsum("td,dkc->kct", normed_low, in_three, preferred_element_type=jnp.float32)
     projected = projected + in_bias.reshape(3, model_width)[:, :, None]
-    received = lax.all_to_all(
-        projected.astype(jnp.bfloat16), "seq", split_axis=1, concat_axis=2, tiled=True
-    )
+    shard = projected.astype(jnp.bfloat16)
+    ways, here = (lax.axis_size("seq"), lax.axis_index("seq"))
+    width = shard.shape[1] // ways
+    dims = list(shard.shape)
+    dims[1] = width
+    height = dims[2]
+    dims[2] = height * ways
+    full = jnp.zeros(dims, shard.dtype)
+    for mask in range(ways):
+        part = lax.dynamic_slice_in_dim(shard, (here ^ mask) * width, width, axis=1)
+        if mask:
+            part = lax.ppermute(part, "seq", [(d, d ^ mask) for d in range(ways)])
+        full = lax.dynamic_update_slice_in_dim(full, part, (here ^ mask) * height, axis=2)
+    received = full
     features = position_features(length)
     count_p, count_q = split_length(2 * length)
     tables = dft_tables(count_p, count_q)

time: 1630 us -> 1580 us (0.969)
  waiting for transfers between devices: 866 us -> 809 us
    all_to_all x1 -> x0, waiting for transfers between devices: 70.4 us -> none  [on_device(): lax.all_to_all(projected.astype(jnp.bfloat16), 'seq', split_axis=1, conca...]
  transfers between devices with their start and end apart: 10 -> 16, of which waited for: 7 -> 7; matrix products, arithmetic and copies ran while one was open for 18% -> 19% of each run, Pallas kernels for 0% -> 0%
where the time goes in v1:
time: 1580 us
  waiting for transfers between devices  809 us (51%)
  matrix products  437 us (28%)
  blocking collectives  188 us (12%)
  local copies, waits for them, and re-layouts  68.5 us (4%)
  other arithmetic  45.2 us (3%)
  starting transfers between devices  17.4 us (1%)
  between operations  15.8 us (1%)
    reduce_scatter x1, waiting for transfers between devices, reduce_matrices(): lax.psum_scatter(matrix_grads[2], 'seq', scatter_dimension=0, tiled=True)  286 us
    reduce_scatter x1, waiting for transfers between devices, reduce_matrices(): lax.psum_scatter(matrix_grads[3], 'seq', scatter_dimension=0, tiled=True)  255 us
    reduce_scatter x1, waiting for transfers between devices, reduce_matrices(): lax.psum_scatter(matrix_grads[0], 'seq', scatter_dimension=0, tiled=True)  177 us
    all_to_all x1, blocking collectives, on_device(): lax.all_to_all(grad_received.astype(jnp.bfloat16), 'seq', split_axis=2, c...  93.1 us
    dot_general x4, matrix products, forward_real(): jnp.einsum('ckn,nm->ckm', turned_re, sin_q, precision=HIGH)  41.6 us
    psum x1, blocking collectives, on_device(): lax.psum((grad_gain1, grad_shift1, grad_in_bias, grad_out_bias, grad_gain...  41.1 us
    all_to_all x1, blocking collectives, on_device(): lax.all_to_all(mixed.astype(jnp.bfloat16), 'seq', split_axis=1, concat_ax...  40.9 us
    dot_general x4, matrix products, forward_real(): jnp.einsum('kn,cnq->ckq', cos_p[:, :half_rows], blocked, precision=HIGH)  38.2 us
  transfers between devices with their start and end apart: 16, of which 7 were waited for; matrix products, arithmetic and copies ran while one was open for 19% of the time, Pallas kernels for 0%

profile of v1, /device:TPU:0, one launch (start us, length us, event | category | flops | bytes accessed | tf_op | source)
XLA Modules:
  0.0 1580.8 jit_solution(4491395435882854591)
XLA Ops:
  50.7 9.5 fusion.127
  75.5 14.0 collective-permute-done.4
  101.3 9.3 fusion.131
  110.6 9.5 fusion.133
  120.2 12.3 fusion.24
  152.4 9.2 fusion.64
  161.6 9.6 fusion.87
  171.2 9.1 fusion.90
  180.3 9.4 fusion.81
  189.7 14.2 multiply_subtract_fusion
  221.4 18.1 %fusion.44 = f32[128,64,64]{0,2,1:T(8,128)S(1)} fusion(f32[128,64]{0,1:T(8,128)S(1)} %get-tuple-element.111, f32[128,64]{0,1:T(8,128)S(1)} %get-tuple-element.112, f32[128,128,64]{1,2,0:T(8,128)S(1)} %fusion.184, f32[128,128,64]{1,2,0:T(8,128)S(1)} %fusion.202, f32[128,128,64]{1,2,0:T(8,128)S(1)} %fusion.182, f32[128,128,64]{1,2,0:T(8,128)S(1)} %fusion.200, ...), kind=kOutput, calls=%fused_computation.88 | convolution fusion | flops 810549248 | bytes 19005440 | tf_op jit(solution)/shard_map/jvp(nk,ckq->cnq)/dot_general | solution.py:93
  239.5 21.2 %multiply_bitcast_fusion = f32[128,64,64]{0,1,2:T(8,128)S(1)} fusion(f32[128,64,64]{0,2,1:T(8,128)S(1)} %fusion.44, f32[128,64]{0,1:T(8,128)S(1)} %get-tuple-element.111, f32[128,64]{0,1:T(8,128)S(1)} %get-tuple-element.112, f32[128,128,64]{1,2,0:T(8,128)S(1)} %fusion.184, f32[128,128,64]{1,2,0:T(8,128)S(1)} %fusion.202, f32[128,128,64]{1,2,0:T(8,128)S(1)} %fusion.182, ...), kind=kOutput, calls=%fused_computation.183 | convolution fusion | flops 811597824 | bytes 21102592 | tf_op jit(solution)/shard_map/jvp(nk,ckq->cnq)/dot_general | solution.py:93
  262.6 40.9 %all_to_all.47 = bf16[128,8,512]{0,2,1:T(8,128)(2,1)} all-to-all(bf16[128,8,512]{0,2,1:T(8,128)(2,1)S(1)} %fusion.118), channel_id=1, replica_groups=mesh['dp'=4,'seq'=8] {'seq'}, dimensions={1} | all-to-all | bytes 2097152 | tf_op jit(solution)/shard_map/all_to_all | solution.py:231
  308.8 10.8 fusion.353
  319.6 16.2 %convert_reduce_fusion = (f32[4096]{0:T(1024)}, bf16[512,4096]{1,0:T(8,128)(2,1)}) fusion(f32[512,4096]{1,0:T(8,128)} %fusion.353, f32[4096]{0:T(1024)S(1)} %copy-done.75, bf16[4096,1024]{1,0:T(8,128)(2,1)} %param.42, bf16[1,512,1024]{2,1,0:T(8,128)(2,1)S(1)} %copy-done.28), kind=kOutput, calls=%fused_computation.9 | convolution fusion | flops 4343197696 | bytes 22052864 | tf_op jit(solution)/shard_map/td,fd->tf/dot_general | solution.py:249
  357.6 36.0 %all-to-all-done.1 = bf16[8,128,512]{1,2,0:T(8,128)(2,1)} async-done(((bf16[8,128,512]{1,2,0:T(8,128)(2,1)}), bf16[8,128,512]{1,2,0:T(8,128)(2,1)}, u32[]{:S(2)}, u32[]{:S(2)}) %all-to-all-start.1) | async-done | bytes 1048608 | tf_op jit(solution)/shard_map/all_to_all | solution.py:268
  418.6 9.6 fusion.38
  428.2 9.3 fusion.96
  437.5 17.6 %multiply_add_fusion.2 = (f32[128,128,64]{1,2,0:T(8,128)S(1)}, f32[128,128,64]{1,2,0:T(8,128)}, f32[128,128,64]{1,2,0:T(8,128)}, f32[128,128,64]{1,2,0:T(8,128)}) fusion(f32[128,128,64]{1,2,0:T(8,128)} %get-tuple-element.103, f32[128,128,64]{1,2,0:T(8,128)} %fusion.81, f32[128,128,64]{1,2,0:T(8,128)} %fusion.96, f32[128,128,64]{1,2,0:T(8,128)} %fusion.87, ...), kind=kOutput, calls=%fused_computation.83 | convolution fusion | flops 820043776 | bytes 46137344 | tf_op jit(solution)/shard_map/transpose(jvp(ckm,nm->ckn))/dot_general | solution.py:88
  490.8 12.2 fusion.14
  503.0 9.3 fusion.32
  541.1 20.0 %copy.241 = bf16[3,128,4096]{1,0,2:T(4,128)(2,1)S(1)} copy(bf16[3,128,4096]{1,2,0:T(8,128)(2,1)S(1)} %fusion.9) | data formatting | bytes 6291456 | tf_op jit(solution)/shard_map/convert_element_type | solution.py:282
  561.1 93.1 %all_to_all.48 = bf16[3,128,4096]{1,0,2:T(4,128)(2,1)S(1)} all-to-all(bf16[3,128,4096]{1,0,2:T(4,128)(2,1)S(1)} %copy.241), channel_id=1, replica_groups=mesh['dp'=4,'seq'=8] {'seq'}, dimensions={2} | all-to-all | bytes 6291456 | tf_op jit(solution)/shard_map/all_to_all | solution.py:281
  670.1 13.3 fusion.352
  683.5 15.8 fusion.144
  700.0 176.7 %reduce-scatter.9.cloned.1.call-done = f32[128,3072]{1,0:T(8,128)} async-done(((f32[1024,3072]{1,0:T(8,128)}), f32[128,3072]{1,0:T(8,128)}) %reduce-scatter.9.cloned.1.call-update) | async-done | bytes 1572880 | tf_op jit(solution)/shard_map/reduce_scatter | solution.py:137
  876.8 286.0 %reduce-scatter.17.cloned.1.call-done = f32[128,4096]{1,0:T(8,128)} async-done(((f32[1024,4096]{1,0:T(8,128)}), f32[128,4096]{1,0:T(8,128)}) %reduce-scatter.17.cloned.1.call-update) | async-done | bytes 2097168 | tf_op jit(solution)/shard_map/reduce_scatter | solution.py:139
  1163.1 13.0 fusion.142
  1192.9 255.3 %reduce-scatter.21.cloned.1.call-done = f32[512,1024]{1,0:T(8,128)} async-done(((f32[4096,1024]{1,0:T(8,128)}), f32[512,1024]{1,0:T(8,128)}) %reduce-scatter.21.cloned.1.call-update) | async-done | bytes 2097168 | tf_op jit(solution)/shard_map/reduce_scatter | solution.py:140
  1460.9 12.7 all-reduce.11
  1492.0 41.1 %all-reduce.10 = (f32[1024]{0:T(1024)}, f32[1024]{0:T(1024)}, f32[3072]{0:T(1024)}, f32[33,64]{1,0:T(8,128)}, f32[64]{0:T(128)}, /*index=5*/f32[64]{0:T(128)}, f...) all-reduce(f32[1024]{0:T(1024)S(1)} %get-tuple-element.29, ...), channel_id=1, replica_groups=mesh['dp'=4,'seq'=8] {'dp','seq'}, use_global_device_ids=true, to_apply=%region_9.10 | all-reduce | flops 15552 | bytes 124416 | tf_op jit(solution)/shard_map/psum | solution.py:291
  1539.2 34.4 %reduce-scatter.23.cloned.1.call-done = f32[512,256]{1,0:T(8,128)} async-done(((f32[512,1024]{1,0:T(8,128)}), f32[512,256]{1,0:T(8,128)}) %reduce-scatter.23.cloned.1.call-update) | async-done | bytes 524304 | tf_op jit(solution)/shard_map/reduce_scatter | solution.py:146
  (301 shorter events, 296.2 us)
Async XLA Ops:
  7.2 298.6 %copy-start = (bf16[1024,1024]{1,0:T(8,128)(2,1)S(1)}, bf16[1024,1024]{1,0:T(8,128)(2,1)}, u32[]{:S(2)}) copy-start(bf16[1024,1024]{1,0:T(8,128)(2,1)} %param.36) | copy-start | bytes 6291460
  29.1 35.5 %collective-permute-start = (bf16[3,128,512]{1,2,0:T(8,128)(2,1)}, bf16[3,128,512]{1,2,0:T(8,128)(2,1)}, u32[]{:S(2)}, u32[]{:S(2)}) collective-permute-start(bf16[3,128,512]{1,2,0:T(8,128)(2,1)} %get-tuple-element.90), channel_id=1, source_target_pairs={{0,1},{1,0},{2,3},{3,2},{4,5},{5,4},{6,7},{7,6},{8,9},{9,8},{10,11... | collective-permute-start | bytes 1179656 | tf_op jit(solution)/shard_map/ppermute | solution.py:196
  32.1 38.0 %collective-permute-start.1 = (bf16[3,128,512]{1,2,0:T(8,128)(2,1)}, bf16[3,128,512]{1,2,0:T(8,128)(2,1)}, u32[]{:S(2)}, u32[]{:S(2)}) collective-permute-start(bf16[3,128,512]{1,2,0:T(8,128)(2,1)} %get-tuple-element.89), channel_id=1, source_target_pairs={{0,2},{1,3},{2,0},{3,1},{4,6},{5,7},{6,4},{7,5},{8,10},{9,11},{10,... | collective-permute-start | bytes 1179656 | tf_op jit(solution)/shard_map/ppermute | solution.py:196
  33.6 38.3 %collective-permute-start.2 = (bf16[3,128,512]{1,2,0:T(8,128)(2,1)}, bf16[3,128,512]{1,2,0:T(8,128)(2,1)}, u32[]{:S(2)}, u32[]{:S(2)}) collective-permute-start(bf16[3,128,512]{1,2,0:T(8,128)(2,1)} %get-tuple-element.88), channel_id=1, source_target_pairs={{0,3},{1,2},{2,1},{3,0},{4,7},{5,6},{6,5},{7,4},{8,11},{9,10},{10,... | collective-permute-start | bytes 1179656 | tf_op jit(solution)/shard_map/ppermute | solution.py:196
  33.6 40.1 %collective-permute-start.3 = (bf16[3,128,512]{1,2,0:T(8,128)(2,1)}, bf16[3,128,512]{1,2,0:T(8,128)(2,1)}, u32[]{:S(2)}, u32[]{:S(2)}) collective-permute-start(bf16[3,128,512]{1,2,0:T(8,128)(2,1)} %get-tuple-element.87), channel_id=1, source_target_pairs={{0,4},{1,5},{2,6},{3,7},{4,0},{5,1},{6,2},{7,3},{8,12},{9,13},{10,... | collective-permute-start | bytes 1179656 | tf_op jit(solution)/shard_map/ppermute | solution.py:196
  36.6 52.9 %collective-permute-start.4 = (bf16[3,128,512]{1,2,0:T(8,128)(2,1)}, bf16[3,128,512]{1,2,0:T(8,128)(2,1)}, u32[]{:S(2)}, u32[]{:S(2)}) collective-permute-start(bf16[3,128,512]{1,2,0:T(8,128)(2,1)} %get-tuple-element.86), channel_id=1, source_target_pairs={{0,5},{1,4},{2,7},{3,6},{4,1},{5,0},{6,3},{7,2},{8,13},{9,12},{10,... | collective-permute-start | bytes 1179656 | tf_op jit(solution)/shard_map/ppermute | solution.py:196
  60.2 35.1 %copy-start.53 = (f32[3,128]{1,0:T(4,128)}, f32[3,128]{1,0:T(4,128)S(1)}, u32[]{:S(2)}) copy-start(f32[3,128]{1,0:T(4,128)S(1)} %get-tuple-element.101) | copy-start | bytes 4612
  60.2 35.1 %copy-start.55 = (f32[3,128]{1,0:T(4,128)}, f32[3,128]{1,0:T(4,128)S(1)}, u32[]{:S(2)}) copy-start(f32[3,128]{1,0:T(4,128)S(1)} %get-tuple-element.100) | copy-start | bytes 4612
  60.3 35.1 %copy-start.57 = (f32[3,128]{1,0:T(4,128)}, f32[3,128]{1,0:T(4,128)S(1)}, u32[]{:S(2)}) copy-start(f32[3,128]{1,0:T(4,128)S(1)} %get-tuple-element.102) | copy-start | bytes 4612
  64.6 26.8 %collective-permute-start.5 = (bf16[3,128,512]{1,2,0:T(8,128)(2,1)}, bf16[3,128,512]{1,2,0:T(8,128)(2,1)S(1)}, u32[]{:S(2)}, u32[]{:S(2)}) collective-permute-start(bf16[3,128,512]{1,2,0:T(8,128)(2,1)} %get-tuple-element.85), channel_id=1, source_target_pairs={{0,6},{1,7},{2,4},{3,5},{4,2},{5,3},{6,0},{7,1},{8,14},{9,15},{10,... | collective-permute-start | bytes 1179656 | tf_op jit(solution)/shard_map/ppermute | solution.py:196
  70.1 22.1 %collective-permute-start.6 = (bf16[3,128,512]{1,2,0:T(8,128)(2,1)}, bf16[3,128,512]{1,2,0:T(8,128)(2,1)S(1)}, u32[]{:S(2)}, u32[]{:S(2)}) collective-permute-start(bf16[3,128,512]{1,2,0:T(8,128)(2,1)} %get-tuple-element.84), channel_id=1, source_target_pairs={{0,7},{1,6},{2,5},{3,4},{4,3},{5,2},{6,1},{7,0},{8,15},{9,14},{10,... | collective-permute-start | bytes 1179656 | tf_op jit(solution)/shard_map/ppermute | solution.py:196
  101.3 160.7 %copy-start.2 = (f32[1,128,4096]{1,2,0:T(8,128)}, f32[1,128,4096]{1,2,0:T(8,128)S(1)}, u32[]{:S(2)}) copy-start(f32[1,128,4096]{1,2,0:T(8,128)S(1)} %get-tuple-element.80) | copy-start | bytes 6291460
  261.9 41.6 %copy-start.18 = (f32[128,64,64]{0,2,1:T(8,128)}, f32[128,64,64]{0,2,1:T(8,128)S(1)}, u32[]{:S(2)}) copy-start(f32[128,64,64]{0,2,1:T(8,128)S(1)} %copy.222) | copy-start | bytes 6291460
  262.3 43.5 %copy-start.43 = (f32[1024]{0:T(1024)S(1)}, f32[1024]{0:T(1024)}, u32[]{:S(2)}) copy-start(f32[1024]{0:T(1024)} %param.37) | copy-start | bytes 12292
  308.4 35.5 %copy-start.15 = (f32[512,1024]{1,0:T(8,128)}, f32[512,1024]{1,0:T(8,128)S(1)}, u32[]{:S(2)}) copy-start(f32[512,1024]{1,0:T(8,128)S(1)} %get-tuple-element.105) | copy-start | bytes 6291460
  308.8 27.1 %slice-start.4 = ((s8[8388608]{0:T(1024)(128)(4,1)}), s8[4194304]{0:T(1024)(128)(4,1)S(1)}, s32[]{:S(2)}) async-start(s8[8388608]{0:T(1024)(128)(4,1)} %bitcast.405), calls=%async_computation.23 | async-start | bytes 8388608
  348.5 45.1 %all-to-all-start.1 = ((bf16[8,128,512]{1,2,0:T(8,128)(2,1)}), bf16[8,128,512]{1,2,0:T(8,128)(2,1)}, u32[]{:S(2)}, u32[]{:S(2)}) async-start(bf16[8,128,512]{1,2,0:T(8,128)(2,1)} %bitcast.377), calls=%async_computation.1 | async-start | bytes 2097152 | tf_op jit(solution)/shard_map/all_to_all | solution.py:268
  352.7 346.7 %reduce-scatter.13.cloned.1.call-start = ((), (), s32[]{:S(2)}) async-start(), calls=%async_computation.13 | async-start | bytes 4718592 | tf_op jit(solution)/shard_map/reduce_scatter | solution.py:138
  357.4 37.6 %copy-start.17 = (f32[1,128,4096]{1,2,0:T(8,128)S(1)}, f32[1,128,4096]{1,2,0:T(8,128)}, u32[]{:S(2)}) copy-start(f32[1,128,4096]{1,2,0:T(8,128)} %get-tuple-element.81) | copy-start | bytes 6291460
  357.4 519.3 %reduce-scatter.9.cloned.1.call-start = ((), (), s32[]{:S(2)}) async-start(), calls=%async_computation.11 | async-start | bytes 14155776 | tf_op jit(solution)/shard_map/reduce_scatter | solution.py:137
  670.1 492.8 %reduce-scatter.17.cloned.1.call-start = ((), (), s32[]{:S(2)}) async-start(), calls=%async_computation.15 | async-start | bytes 18874368 | tf_op jit(solution)/shard_map/reduce_scatter | solution.py:139
  683.5 764.7 %reduce-scatter.21.cloned.1.call-start = ((), (), s32[]{:S(2)}) async-start(), calls=%async_computation.17 | async-start | bytes 18874368 | tf_op jit(solution)/shard_map/reduce_scatter | solution.py:140
  699.3 463.7 %copy-start.79 = (f32[1024]{0:T(1024)S(1)}, f32[1024]{0:T(1024)}, u32[]{:S(2)}) copy-start(f32[1024]{0:T(1024)} %param.43) | copy-start | bytes 12292
  699.4 833.7 %reduce-scatter.15.cloned.1.call-start = ((), (), s32[]{:S(2)}) async-start(), calls=%async_computation.14 | async-start | bytes 655360 | tf_op jit(solution)/shard_map/reduce_scatter | solution.py:144
  699.9 833.1 %reduce-scatter.11.cloned.1.call-start = ((), (), s32[]{:S(2)}) async-start(), calls=%async_computation.12 | async-start | bytes 1966080 | tf_op jit(solution)/shard_map/reduce_scatter | solution.py:143
  876.7 662.5 %reduce-scatter.19.cloned.1.call-start = ((), (), s32[]{:S(2)}) async-start(), calls=%async_computation.16 | async-start | bytes 2621440 | tf_op jit(solution)/shard_map/reduce_scatter | solution.py:145
  1162.9 410.8 %reduce-scatter.23.cloned.1.call-start = ((), (), s32[]{:S(2)}) async-start(), calls=%async_computation.18 | async-start | bytes 2621440 | tf_op jit(solution)/shard_map/reduce_scatter | solution.py:146
  1190.3 257.9 %copy-start.40 = (f32[4096]{0:T(1024)S(1)}, f32[4096]{0:T(1024)}, u32[]{:S(2)}) copy-start(f32[4096]{0:T(1024)} %copy-done.39) | copy-start | bytes 49156
  1190.3 257.9 %copy-start.71 = (f32[128]{0:T(128)S(1)}, f32[128]{0:T(128)}, u32[]{:S(2)}) copy-start(f32[128]{0:T(128)} %copy-done.70) | copy-start | bytes 1540
  1192.9 258.7 %copy-start.65 = (f32[64]{0:T(128)S(1)}, f32[64]{0:T(128)}, u32[]{:S(2)}) copy-start(f32[64]{0:T(128)} %param.32) | copy-start | bytes 772
  1458.4 22.6 %copy-start.33 = (f32[16,4096]{1,0:T(8,128)S(1)}, f32[16,4096]{1,0:T(8,128)}, u32[]{:S(2)}) copy-start(f32[16,4096]{1,0:T(8,128)} %copy-done.32) | copy-start | bytes 786436
  1489.2 84.5 %copy-start.1 = (bf16[1024,1024]{1,0:T(8,128)(2,1)S(1)}, bf16[1024,1024]{1,0:T(8,128)(2,1)}, u32[]{:S(2)}) copy-start(bf16[1024,1024]{1,0:T(8,128)(2,1)} %param.36) | copy-start | bytes 6291460
  (71 other events, 512.2 us)
Sparse Core Ops, SparseCore 0:
  357.5 97.4 reduce-scatter.12
  670.2 206.4 reduce-scatter.8
  881.0 281.8 reduce-scatter.16
  1166.5 281.6 reduce-scatter.20
  1451.2 21.1 reduce-scatter.14
  1475.4 28.4 reduce-scatter.10
  1507.1 32.0 reduce-scatter.18
  1542.3 31.2 reduce-scatter.22
